TPU v7x, 32 devices: a whole 2x2x4 slice. The times are simulated.
32 devices in a mesh: dp: 4 (over y, x), row: 4 (over z), col: 2 (over core).
Axes of the slice: x: 2, y: 2, z: 4, core: 2. Of those that a mesh axis runs over, the one named last changes fastest.
Arguments:
- images: bfloat16 [32, 577, 1024], P(('dp', 'row'), None, 'col'), may hold values from -6 to 6
- cotangent: bfloat16 [32, 577, 1024], P(('dp', 'row'), None, 'col'), may hold values from -6 to 6
- micro_batch: int32 [32], P(('dp', 'row')), may hold values from 0 to 1, as said below
- heads_weight: bfloat16 [1024, 3, 1024], P('row', None, 'col'), may hold values from -0.1875 to 0.1875
- heads_bias: bfloat16 [2, 1024], P(None, 'col'), may hold values from -3 to 3
- merge_weight: bfloat16 [1024, 1024], P('col', 'row'), may hold values from -2 to 2
- merge_bias: bfloat16 [1024], P('col'), may hold values from -3 to 3
- expand_weight: bfloat16 [1024, 4096], P('row', 'col'), may hold values from -0.1875 to 0.1875
- expand_bias: bfloat16 [4096], P('col'), may hold values from -3 to 3
- shrink_weight: bfloat16 [4096, 1024], P('col', 'row'), may hold values from -0.09375 to 0.09375
- shrink_bias: bfloat16 [1024], P('col'), may hold values from -3 to 3
- norm_gains: bfloat16 [2, 1024], P(None, 'col'), may hold values from 0.5 to 1.5
- norm_shifts: bfloat16 [2, 1024], P(None, 'col'), may hold values from -2 to 2
Outputs:
- block_out: bfloat16 [32, 577, 1024], P(('dp', 'row'), None, 'col')
- input_grad: float32 [32, 577, 1024], P(('dp', 'row'), None, 'col')
- heads_weight_grad: float32 [1024, 3, 1024], P('row', None, 'col')
- heads_bias_grad: float32 [2, 1024], P(None, 'col')
- merge_weight_grad: float32 [1024, 1024], P('col', 'row')
- merge_bias_grad: float32 [1024], P('col')
- expand_weight_grad: float32 [1024, 4096], P('row', 'col')
- expand_bias_grad: float32 [4096], P('col')
- shrink_weight_grad: float32 [4096, 1024], P('col', 'row')
- shrink_bias_grad: float32 [1024], P('col')
- norm_gains_grad: float32 [2, 1024], P(None, 'col')
- norm_shifts_grad: float32 [2, 1024], P(None, 'col')
Inputs may be any that keep to these rules, and one draw needn't show every extreme that they name: `micro_batch`: every micro-batch number 0 to 1 belongs to at least one image.
All inputs are finite; a program needn't handle non-finite values.
Results may differ from a plain program's by a relative error of at most 0.018.
Values may be sent and summed in bfloat16 or wider, within the bound.
No kernel may reach another device: no remote copies, remote signals or barrier semaphores. Data moves between devices by JAX's collectives and lax.ppermute only.
A program may use at most 192 MiB of HBM per device.

v0:
```python
import jax
import jax.numpy as jnp
from jax import lax
from jax.sharding import PartitionSpec as P

HEAD_DIM = 64
MICRO = 2


def merged(value, axis, join):
    pieces = jax.tree.map(lambda part: lax.all_gather(part, axis), value)
    head = jax.tree.map(lambda part: part[0], pieces)
    tail = jax.tree.map(lambda part: part[1:], pieces)
    subtotal, _ = lax.scan(lambda subtotal, share: (join(subtotal, share), None), head, tail)
    return subtotal


def moments_join(first, second):
    count_sum = first[0] + second[0]
    offset = second[1] - first[1]
    joined_mean = first[1] + offset * (second[0] / count_sum)
    joined_spread = first[2] + second[2] + offset * offset * (first[0] * second[0] / count_sum)
    return (count_sum, joined_mean, joined_spread)


def norm_split(values, gain, shift, full_width):
    local_mean = jnp.mean(values, axis=1)
    local_spread = jnp.sum(jnp.square(values - local_mean[:, None]), axis=1)
    local_count = jnp.full(local_mean.shape, values.shape[1], jnp.float32)
    merged_count, row_mean, row_spread = merged(
        (local_count, local_mean, local_spread), "col", moments_join
    )
    inverse = lax.rsqrt(row_spread / full_width + 1e-05)
    centered = (values - row_mean[:, None]) * inverse[:, None]
    normed = (centered * gain + shift).astype(jnp.bfloat16)
    return (lax.all_gather(normed, "col", axis=1, tiled=True), centered, inverse)


def norm_back_split(partial_rows, centered, inverse, gain, full_width):
    summed = lax.psum_scatter(
        partial_rows.astype(jnp.bfloat16), "col", scatter_dimension=1, tiled=True
    ).astype(jnp.float32)
    scaled = summed * gain
    first_total, second_total = lax.psum(
        (jnp.sum(scaled, axis=1), jnp.sum(scaled * centered, axis=1)), "col"
    )
    result = inverse[:, None] * (
        scaled - first_total[:, None] / full_width - centered * (second_total[:, None] / full_width)
    )
    return (result, jnp.sum(summed * centered, axis=0), jnp.sum(summed, axis=0))


def gather_grads(values):
    return lax.all_gather(values, "col", axis=1, tiled=True)


def branch_split(partial_rows):
    return lax.psum_scatter(
        partial_rows.astype(jnp.bfloat16), "col", scatter_dimension=1, tiled=True
    ).astype(jnp.float32)


def attend(query_low, key_low, value_low):
    scores = jnp.einsum("qhe,khe->hqk", query_low, key_low, preferred_element_type=jnp.float32)
    log_total = jax.nn.logsumexp(scores, axis=-1)
    probabilities = jnp.exp(scores - log_total[..., None]).astype(jnp.bfloat16)
    attended = jnp.einsum(
        "hqk,khe->qhe", probabilities, value_low, preferred_element_type=jnp.float32
    )
    return (attended, log_total)


def attend_back(query_low, key_low, value_low, log_total, upstream):
    scores = jnp.einsum("qhe,khe->hqk", query_low, key_low, preferred_element_type=jnp.float32)
    probabilities = jnp.exp(scores - log_total[..., None])
    probs_low = probabilities.astype(jnp.bfloat16)
    value_grad = jnp.einsum(
        "hqk,qhe->khe", probs_low, upstream, preferred_element_type=jnp.float32
    ).astype(jnp.bfloat16)
    prob_grad = jnp.einsum("qhe,khe->hqk", upstream, value_low, preferred_element_type=jnp.float32)
    score_grad = (
        probabilities * (prob_grad - jnp.sum(prob_grad * probabilities, axis=-1, keepdims=True))
    ).astype(jnp.bfloat16)
    query_grad = jnp.einsum(
        "hqk,khe->qhe", score_grad, key_low, preferred_element_type=jnp.float32
    ).astype(jnp.bfloat16)
    key_grad = jnp.einsum(
        "hqk,qhe->khe", score_grad, query_low, preferred_element_type=jnp.float32
    ).astype(jnp.bfloat16)
    return (query_grad, key_grad, value_grad)


def own_slice(values, col_start, local_width):
    return lax.dynamic_slice_in_dim(values, col_start, local_width, 1)


def shards(
    images,
    cotangent,
    micro_batch,
    heads_weight,
    heads_bias,
    merge_weight,
    merge_bias,
    expand_weight,
    expand_bias,
    shrink_weight,
    shrink_bias,
    norm_gains,
    norm_shifts,
):
    local_width = images.shape[2]
    full_width = local_width * lax.axis_size("col")
    col_start = lax.axis_index("col") * local_width
    local_heads = local_width // HEAD_DIM
    length = images.shape[1]
    slot_count = images.shape[0]
    heads_full, merge_full, expand_full, shrink_full = (
        lax.all_gather(heads_weight, "row", axis=0, tiled=True),
        lax.all_gather(merge_weight, "row", axis=1, tiled=True),
        lax.all_gather(expand_weight, "row", axis=0, tiled=True),
        lax.all_gather(shrink_weight, "row", axis=1, tiled=True),
    )
    member = (micro_batch[:, None] == jnp.arange(MICRO, dtype=jnp.int32)[None, :]).astype(jnp.int32)
    totals = lax.psum(jnp.sum(member, axis=0), ("dp", "row"))
    all_slots = slot_count * lax.axis_size("dp") * lax.axis_size("row")
    batch_weight = all_slots / (MICRO * totals.astype(jnp.float32))
    slot_weight = jnp.sum(member.astype(jnp.float32) * batch_weight[None, :], axis=1)
    gains_own = norm_gains.astype(jnp.float32)
    shifts_own = norm_shifts.astype(jnp.float32)
    heads_bias_own = heads_bias.astype(jnp.float32)
    merge_bias_own = merge_bias.astype(jnp.float32)
    expand_bias_own = expand_bias.astype(jnp.float32)
    shrink_bias_own = shrink_bias.astype(jnp.float32)
    heads_grad = jnp.zeros(heads_full.shape, jnp.float32)
    merge_grad = jnp.zeros(merge_full.shape, jnp.float32)
    expand_grad = jnp.zeros(expand_full.shape, jnp.float32)
    shrink_grad = jnp.zeros(shrink_full.shape, jnp.float32)
    heads_bias_grad = jnp.zeros(heads_bias.shape, jnp.float32)
    merge_bias_grad = jnp.zeros(merge_bias.shape, jnp.float32)
    expand_bias_grad = jnp.zeros(expand_bias.shape, jnp.float32)
    shrink_bias_grad = jnp.zeros(shrink_bias.shape, jnp.float32)
    gain_grad = jnp.zeros(norm_gains.shape, jnp.float32)
    shift_grad = jnp.zeros(norm_shifts.shape, jnp.float32)
    outputs = []
    input_grads = []
    for slot_index in range(slot_count):
        own_input = images[slot_index].astype(jnp.float32)
        weight_now = slot_weight[slot_index]
        normed, centered_one, inverse_one = norm_split(
            own_input, gains_own[0], shifts_own[0], full_width
        )
        mixed_heads = jnp.einsum(
            "td,dkf->tkf", normed, heads_full, preferred_element_type=jnp.float32
        )
        query_low = (
            ((mixed_heads[:, 0] + heads_bias_own[0]) * HEAD_DIM ** (-0.5))
            .astype(jnp.bfloat16)
            .reshape(length, local_heads, HEAD_DIM)
        )
        key_low = mixed_heads[:, 1].astype(jnp.bfloat16).reshape(length, local_heads, HEAD_DIM)
        value_low = (
            (mixed_heads[:, 2] + heads_bias_own[1])
            .astype(jnp.bfloat16)
            .reshape(length, local_heads, HEAD_DIM)
        )
        attended, log_total = attend(query_low, key_low, value_low)
        attended_low = attended.reshape(length, local_width).astype(jnp.bfloat16)
        merge_part = jnp.dot(attended_low, merge_full, preferred_element_type=jnp.float32)
        middle_own = own_input + (branch_split(merge_part) + merge_bias_own)
        normed_two, centered_two, inverse_two = norm_split(
            middle_own, gains_own[1], shifts_own[1], full_width
        )
        hidden = (
            jnp.dot(normed_two, expand_full, preferred_element_type=jnp.float32) + expand_bias_own
        )
        sigmoid_gate = jax.nn.sigmoid(1.702 * hidden)
        activated = (hidden * sigmoid_gate).astype(jnp.bfloat16)
        shrink_part = jnp.dot(activated, shrink_full, preferred_element_type=jnp.float32)
        outputs.append(
            (middle_own + (branch_split(shrink_part) + shrink_bias_own)).astype(jnp.bfloat16)
        )
        cot_full = gather_grads(cotangent[slot_index])
        seed_full = cot_full.astype(jnp.float32) * weight_now
        seed_low = seed_full.astype(jnp.bfloat16)
        seed_own = own_slice(seed_full, col_start, local_width)
        shrink_bias_grad = shrink_bias_grad + jnp.sum(
            own_slice(seed_low, col_start, local_width).astype(jnp.float32), axis=0
        )
        shrink_grad = shrink_grad + jnp.einsum(
            "tf,td->fd", activated, seed_low, preferred_element_type=jnp.float32
        )
        act_grad = jnp.einsum(
            "td,fd->tf", seed_low, shrink_full, preferred_element_type=jnp.float32
        )
        derivative = sigmoid_gate + 1.702 * hidden * sigmoid_gate * (1.0 - sigmoid_gate)
        hidden_grad = (act_grad * derivative).astype(jnp.bfloat16)
        expand_bias_grad = expand_bias_grad + jnp.sum(hidden_grad.astype(jnp.float32), axis=0)
        expand_grad = expand_grad + jnp.einsum(
            "td,tf->df", normed_two, hidden_grad, preferred_element_type=jnp.float32
        )
        norm_part = jnp.einsum(
            "tf,df->td", hidden_grad, expand_full, preferred_element_type=jnp.float32
        )
        norm_result, gain_sum, shift_sum = norm_back_split(
            norm_part, centered_two, inverse_two, gains_own[1], full_width
        )
        middle_grad = seed_own + norm_result
        branch_grad = gather_grads(middle_grad.astype(jnp.bfloat16))
        gain_grad = gain_grad.at[1].add(gain_sum)
        shift_grad = shift_grad.at[1].add(shift_sum)
        merge_bias_grad = merge_bias_grad + jnp.sum(
            own_slice(branch_grad, col_start, local_width).astype(jnp.float32), axis=0
        )
        merge_grad = merge_grad + jnp.einsum(
            "tf,td->fd", attended_low, branch_grad, preferred_element_type=jnp.float32
        )
        attended_grad = (
            jnp.einsum("td,fd->tf", branch_grad, merge_full, preferred_element_type=jnp.float32)
            .astype(jnp.bfloat16)
            .reshape(length, local_heads, HEAD_DIM)
        )
        query_grad, key_grad, value_grad = attend_back(
            query_low, key_low, value_low, log_total, attended_grad
        )
        mixed_grad = jnp.stack(
            [
                query_grad.reshape(length, local_width).astype(jnp.float32) * HEAD_DIM ** (-0.5),
                key_grad.reshape(length, local_width).astype(jnp.float32),
                value_grad.reshape(length, local_width).astype(jnp.float32),
            ],
            axis=1,
        ).astype(jnp.bfloat16)
        heads_bias_grad = heads_bias_grad + jnp.stack(
            [
                jnp.sum(mixed_grad[:, 0].astype(jnp.float32), axis=0),
                jnp.sum(mixed_grad[:, 2].astype(jnp.float32), axis=0),
            ]
        )
        heads_grad = heads_grad + jnp.einsum(
            "td,tkf->dkf", normed, mixed_grad, preferred_element_type=jnp.float32
        )
        first_part = jnp.einsum(
            "tkf,dkf->td", mixed_grad, heads_full, preferred_element_type=jnp.float32
        )
        norm_result, gain_sum, shift_sum = norm_back_split(
            first_part, centered_one, inverse_one, gains_own[0], full_width
        )
        input_grads.append(middle_grad + norm_result)
        gain_grad = gain_grad.at[0].add(gain_sum)
        shift_grad = shift_grad.at[0].add(shift_sum)
    weight_sums = (
        lax.psum_scatter(
            heads_grad.astype(jnp.bfloat16), "row", scatter_dimension=0, tiled=True
        ).astype(jnp.float32),
        lax.psum_scatter(
            merge_grad.astype(jnp.bfloat16), "row", scatter_dimension=1, tiled=True
        ).astype(jnp.float32),
        lax.psum_scatter(
            expand_grad.astype(jnp.bfloat16), "row", scatter_dimension=0, tiled=True
        ).astype(jnp.float32),
        lax.psum_scatter(
            shrink_grad.astype(jnp.bfloat16), "row", scatter_dimension=1, tiled=True
        ).astype(jnp.float32),
    )
    weight_sums = (
        lax.psum(weight_sums[0].astype(jnp.bfloat16), "dp").astype(jnp.float32),
        lax.psum(weight_sums[1].astype(jnp.bfloat16), "dp").astype(jnp.float32),
        lax.psum(weight_sums[2].astype(jnp.bfloat16), "dp").astype(jnp.float32),
        lax.psum(weight_sums[3].astype(jnp.bfloat16), "dp").astype(jnp.float32),
    )
    small_totals = lax.psum(
        (
            heads_bias_grad,
            merge_bias_grad,
            expand_bias_grad,
            shrink_bias_grad,
            gain_grad,
            shift_grad,
        ),
        ("dp", "row"),
    )
    return (
        jnp.stack(outputs),
        jnp.stack(input_grads),
        weight_sums[0],
        small_totals[0],
        weight_sums[1],
        small_totals[1],
        weight_sums[2],
        small_totals[2],
        weight_sums[3],
        small_totals[3],
        small_totals[4],
        small_totals[5],
    )


def solution(mesh):
    placed = (
        P(("dp", "row"), None, "col"),
        P(("dp", "row"), None, "col"),
        P(("dp", "row")),
        P("row", None, "col"),
        P(None, "col"),
        P("col", "row"),
        P("col"),
        P("row", "col"),
        P("col"),
        P("col", "row"),
        P("col"),
        P(None, "col"),
        P(None, "col"),
    )
    return jax.shard_map(
        shards,
        mesh=mesh,
        in_specs=placed,
        out_specs=(
            P(("dp", "row"), None, "col"),
            P(("dp", "row"), None, "col"),
            P("row", None, "col"),
            P(None, "col"),
            P("col", "row"),
            P("col"),
            P("row", "col"),
            P("col"),
            P("col", "row"),
            P("col"),
            P(None, "col"),
            P(None, "col"),
        ),
        check_vma=False,
    )
```

profile of v0, /device:TPU:0, one launch (start us, length us, event | category | flops | bytes accessed | tf_op | source)
XLA Modules:
  0.0 845.2 jit_solution(18113840407815767616)
XLA Ops:
  26.4 9.3 %all-gather.35.cloned.1.call-done = bf16[577,1024]{1,0:T(8,128)(2,1)} async-done(((bf16[577,512]{1,0:T(8,128)(2,1)}), bf16[577,1024]{1,0:T(8,128)(2,1)}) %all-gather.35.cloned.1.call-update) | async-done | bytes 1181712 | tf_op jit(solution)/shard_map/all_gather | solution.py:36
  35.7 66.2 %all-gather.25.cloned.1.call-done = bf16[1024,3,512]{2,0,1:T(8,128)(2,1)} async-done(((bf16[256,3,512]{2,0,1:T(8,128)(2,1)}), bf16[1024,3,512]{2,0,1:T(8,128)(2,1)}) %all-gather.25.cloned.1.call-update) | async-done | bytes 3145744 | tf_op jit(solution)/shard_map/all_gather | solution.py:119
  122.0 6.5 fusion.145
  138.0 6.2 exponential_reduce_fusion
  186.0 14.7 %psum.133 = s32[2]{0:T(128)S(1)} all-reduce(s32[2]{0:T(128)S(1)} %fusion.120), channel_id=1, replica_groups=mesh['dp'=4,'row'=4,'col'=2] {'dp','row'}, use_global_device_ids=true, to_apply=%region_17.18 | all-reduce | flops 2 | bytes 16 | tf_op jit(solution)/shard_map/psum | solution.py:125
  210.0 74.1 %all-gather.31.cloned.1.call-done = bf16[1024,2048]{1,0:T(8,128)(2,1)} async-done(((bf16[256,2048]{1,0:T(8,128)(2,1)}), bf16[1024,2048]{1,0:T(8,128)(2,1)}) %all-gather.31.cloned.1.call-update) | async-done | bytes 4194320 | tf_op jit(solution)/shard_map/all_gather | solution.py:121
  284.1 9.2 %all-gather.37.cloned.1.call-done = bf16[577,1024]{1,0:T(8,128)(2,1)} async-done(((bf16[577,512]{1,0:T(8,128)(2,1)}), bf16[577,1024]{1,0:T(8,128)(2,1)}) %all-gather.37.cloned.1.call-update) | async-done | bytes 1181712 | tf_op jit(solution)/shard_map/all_gather | solution.py:36
  293.3 7.4 fusion.147
  300.7 75.9 %all-gather.33.cloned.1.call-done = bf16[2048,1024]{1,0:T(8,128)(2,1)} async-done(((bf16[2048,256]{1,0:T(8,128)(2,1)}), bf16[2048,1024]{1,0:T(8,128)(2,1)}) %all-gather.33.cloned.1.call-update) | async-done | bytes 4194320 | tf_op jit(solution)/shard_map/all_gather | solution.py:122
  376.6 8.6 %convert_reduce_fusion = (f32[2048]{0:T(1024)}, bf16[577,2048]{1,0:T(8,128)(2,1)S(1)}) fusion(f32[577,2048]{1,0:T(8,128)} %fusion.147, f32[2048]{0:T(1024)S(1)} %convert_element_type.388, bf16[2048,1024]{1,0:T(8,128)(2,1)} %all-gather.33.cloned.1.call-done, bf16[1,577,1024]{2,1,0:T(8,128)(2,1)} %get-tuple-element.297), kind=kOutput, calls=%fused_computation.13 | convolution fusion | flops 2435473408 | bytes 12482560 | tf_op jit(solution)/shard_map/td,fd->tf/dot_general | solution.py:193
  405.8 7.4 convolution_convert_fusion.4
  413.3 7.3 convolution_convert_fusion.2
  440.6 8.7 %all-gather.39.cloned.1.call-done = bf16[577,1024]{1,0:T(8,128)(2,1)} async-done(((bf16[577,512]{1,0:T(8,128)(2,1)}), bf16[577,1024]{1,0:T(8,128)(2,1)}) %all-gather.39.cloned.1.call-update) | async-done | bytes 1181712 | tf_op jit(solution)/shard_map/all_gather | solution.py:54
  453.1 8.1 all-gather.41.cloned.1.call-done
  470.9 8.0 add_convert_fusion
  498.4 7.3 fusion.31
  506.9 7.3 fusion.37
  522.4 6.1 multiply_convert_fusion
  545.1 6.2 multiply_convert_fusion.1
  585.3 65.7 %reduce-scatter.33.cloned.1.call-done = bf16[256,2048]{1,0:T(8,128)(2,1)} async-done(((bf16[1024,2048]{1,0:T(8,128)(2,1)}), bf16[256,2048]{1,0:T(8,128)(2,1)}) %reduce-scatter.33.cloned.1.call-update) | async-done | bytes 1048592 | tf_op jit(solution)/shard_map/reduce_scatter | solution.py:259
  651.0 63.2 %reduce-scatter.29.cloned.1.call-done = bf16[256,3,512]{2,0,1:T(8,128)(2,1)} async-done(((bf16[1024,3,512]{2,0,1:T(8,128)(2,1)}), bf16[256,3,512]{2,0,1:T(8,128)(2,1)}) %reduce-scatter.29.cloned.1.call-update) | async-done | bytes 786448 | tf_op jit(solution)/shard_map/reduce_scatter | solution.py:253
  716.8 9.0 %reduce-scatter.27.cloned.1.call-done = bf16[577,512]{1,0:T(8,128)(2,1)} async-done(((bf16[577,1024]{1,0:T(8,128)(2,1)}), bf16[577,512]{1,0:T(8,128)(2,1)}) %reduce-scatter.27.cloned.1.call-update) | async-done | bytes 590864 | tf_op jit(solution)/shard_map/reduce_scatter | solution.py:40
  725.8 12.6 %reduce-scatter.23.cloned.1.call-done = bf16[577,512]{1,0:T(8,128)(2,1)} async-done(((bf16[577,1024]{1,0:T(8,128)(2,1)}), bf16[577,512]{1,0:T(8,128)(2,1)}) %reduce-scatter.23.cloned.1.call-update) | async-done | bytes 590864 | tf_op jit(solution)/shard_map/reduce_scatter | solution.py:40
  750.3 78.3 %all-reduce.8 = (f32[2,512]{1,0:T(2,128)}, f32[512]{0:T(512)}, f32[2048]{0:T(1024)}, f32[512]{0:T(512)}, f32[2,512]{1,0:T(2,128)}, /*index=5*/f32[2,512]{1,0:T(2,128)}) all-reduce(f32[2,512]{1,0:T(2,128)S(1)} %maximum_add_fusion, f32[512]{0:T(512)S(1)} %add.530, ...), channel_id=1, replica_groups=mesh['dp'=4,'row'=4,'col'=2] {'dp','row'}, use_global_device_ids=true, to_apply=%region_47.48 | all-reduce | flops 6144 | bytes 49152 | tf_op jit(solution)/shard_map/psum | solution.py:272
  (359 shorter events, 255.4 us)
Async XLA Ops:
  7.2 28.5 %all-gather.35.cloned.1.call-start = ((), (), s32[]{:S(2)}) async-start(), calls=%async_computation.20 | async-start | bytes 1794048 | tf_op jit(solution)/shard_map/all_gather | solution.py:36
  23.9 78.1 %all-gather.25.cloned.1.call-start = ((), (), s32[]{:S(2)}) async-start(), calls=%async_computation.13 | async-start | bytes 3932160 | tf_op jit(solution)/shard_map/all_gather | solution.py:119
  24.6 87.4 %all-gather.23.cloned.1.call-start = ((), (), s32[]{:S(2)}) async-start(), calls=%async_computation.12 | async-start | bytes 1794048 | tf_op jit(solution)/shard_map/all_gather | solution.py:36
  25.3 124.7 %all-gather.27.cloned.1.call-start = ((), (), s32[]{:S(2)}) async-start(), calls=%async_computation.14 | async-start | bytes 1310720 | tf_op jit(solution)/shard_map/all_gather | solution.py:120
  25.9 147.2 %reduce-scatter.17.cloned.1.call-start = ((), (), s32[]{:S(2)}) async-start(), calls=%async_computation.21 | async-start | bytes 1794048 | tf_op jit(solution)/shard_map/reduce_scatter | solution.py:58
  153.4 23.1 %reduce-scatter.13.cloned.1.call-start = ((), (), s32[]{:S(2)}) async-start(), calls=%async_computation.15 | async-start | bytes 1794048 | tf_op jit(solution)/shard_map/reduce_scatter | solution.py:58
  166.5 35.0 %all-gather.43.cloned.1.call-start = ((), (), s32[]{:S(2)}) async-start(), calls=%async_computation.34 | async-start | bytes 1794048 | tf_op jit(solution)/shard_map/all_gather | solution.py:54
  171.2 34.5 %all-gather.45.cloned.1.call-start = ((), (), s32[]{:S(2)}) async-start(), calls=%async_computation.35 | async-start | bytes 1794048 | tf_op jit(solution)/shard_map/all_gather | solution.py:54
  172.3 111.8 %all-gather.31.cloned.1.call-start = ((), (), s32[]{:S(2)}) async-start(), calls=%async_computation.17 | async-start | bytes 5242880 | tf_op jit(solution)/shard_map/all_gather | solution.py:121
  173.0 120.3 %all-gather.37.cloned.1.call-start = ((), (), s32[]{:S(2)}) async-start(), calls=%async_computation.22 | async-start | bytes 1794048 | tf_op jit(solution)/shard_map/all_gather | solution.py:36
  185.2 191.4 %all-gather.33.cloned.1.call-start = ((), (), s32[]{:S(2)}) async-start(), calls=%async_computation.18 | async-start | bytes 5242880 | tf_op jit(solution)/shard_map/all_gather | solution.py:122
  185.9 204.9 %all-gather.29.cloned.1.call-start = ((), (), s32[]{:S(2)}) async-start(), calls=%async_computation.16 | async-start | bytes 1794048 | tf_op jit(solution)/shard_map/all_gather | solution.py:36
  210.0 210.8 %reduce-scatter.25.cloned.1.call-start = ((), (), s32[]{:S(2)}) async-start(), calls=%async_computation.27 | async-start | bytes 1794048 | tf_op jit(solution)/shard_map/reduce_scatter | solution.py:40
  390.5 30.2 %reduce-scatter.21.cloned.1.call-start = ((), (), s32[]{:S(2)}) async-start(), calls=%async_computation.24 | async-start | bytes 1794048 | tf_op jit(solution)/shard_map/reduce_scatter | solution.py:40
  413.2 23.7 %reduce-scatter.19.cloned.1.call-start = ((), (), s32[]{:S(2)}) async-start(), calls=%async_computation.23 | async-start | bytes 1794048 | tf_op jit(solution)/shard_map/reduce_scatter | solution.py:58
  420.6 28.7 %all-gather.39.cloned.1.call-start = ((), (), s32[]{:S(2)}) async-start(), calls=%async_computation.25 | async-start | bytes 1794048 | tf_op jit(solution)/shard_map/all_gather | solution.py:54
  431.2 30.0 %all-gather.41.cloned.1.call-start = ((), (), s32[]{:S(2)}) async-start(), calls=%async_computation.28 | async-start | bytes 1794048 | tf_op jit(solution)/shard_map/all_gather | solution.py:54
  440.6 144.7 %reduce-scatter.31.cloned.1.call-start = ((), (), s32[]{:S(2)}) async-start(), calls=%async_computation.31 | async-start | bytes 1310720 | tf_op jit(solution)/shard_map/reduce_scatter | solution.py:256
  465.2 120.1 %reduce-scatter.35.cloned.1.call-start = ((), (), s32[]{:S(2)}) async-start(), calls=%async_computation.33 | async-start | bytes 5242880 | tf_op jit(solution)/shard_map/reduce_scatter | solution.py:262
  479.0 172.0 %reduce-scatter.33.cloned.1.call-start = ((), (), s32[]{:S(2)}) async-start(), calls=%async_computation.32 | async-start | bytes 5242880 | tf_op jit(solution)/shard_map/reduce_scatter | solution.py:259
  490.2 223.9 %reduce-scatter.29.cloned.1.call-start = ((), (), s32[]{:S(2)}) async-start(), calls=%async_computation.30 | async-start | bytes 3932160 | tf_op jit(solution)/shard_map/reduce_scatter | solution.py:253
  569.1 156.7 %reduce-scatter.27.cloned.1.call-start = ((), (), s32[]{:S(2)}) async-start(), calls=%async_computation.29 | async-start | bytes 1794048 | tf_op jit(solution)/shard_map/reduce_scatter | solution.py:40
  574.6 163.8 %reduce-scatter.23.cloned.1.call-start = ((), (), s32[]{:S(2)}) async-start(), calls=%async_computation.26 | async-start | bytes 1794048 | tf_op jit(solution)/shard_map/reduce_scatter | solution.py:40
  580.0 251.9 %all-reduce.16.cloned.1.call-start = ((), (), s32[]{:S(2)}) async-start(), calls=%async_computation.36 | async-start | bytes 6291456 | tf_op jit(solution)/shard_map/psum | solution.py:267
  (76 other events, 659.8 us)
Sparse Core Ops, SparseCore 0:
  24.0 11.6 all-gather.34
  37.3 64.6 all-gather.24
  104.0 7.9 all-gather.22
  113.4 31.3 all-gather.26
  153.5 9.7 reduce-scatter.16
  166.7 9.8 reduce-scatter.12
  178.1 10.4 all-gather.42
  190.1 10.4 all-gather.44
  202.1 81.9 all-gather.30
  285.5 7.7 all-gather.36
  294.8 81.7 all-gather.32
  378.6 7.4 all-gather.28
  390.6 7.4 reduce-scatter.24
  414.9 9.8 reduce-scatter.14
  427.0 9.8 reduce-scatter.18
  438.9 10.4 all-gather.38
  450.8 10.4 all-gather.40
  465.3 28.3 reduce-scatter.30
  495.9 75.4 reduce-scatter.34
  573.7 77.2 reduce-scatter.32
  653.4 60.7 reduce-scatter.28
  717.1 8.6 reduce-scatter.26
  728.5 9.8 reduce-scatter.22
  742.1 89.7 all-reduce.15
  (1 shorter events, 6.8 us)
where the time goes:
time: 851 us; the launch traced here: 845 us
  waiting for transfers between devices  422 us (50%)
  matrix products  174 us (20%)
  blocking collectives  107 us (13%)
  other arithmetic  63.1 us (7%)
  local copies, waits for them, and re-layouts  60.1 us (7%)
  between operations  16.3 us (2%)
    psum x1, blocking collectives, shards(): lax.psum((heads_bias_grad, merge_bias_grad, expand_bias_grad, shrink_bias...  78.3 us
    all_gather x1, waiting for transfers between devices, shards(): lax.all_gather(shrink_weight, 'row', axis=1, tiled=True)  75.9 us
    all_gather x1, waiting for transfers between devices, shards(): lax.all_gather(expand_weight, 'row', axis=0, tiled=True)  74.1 us
    all_gather x1, waiting for transfers between devices, shards(): lax.all_gather(heads_weight, 'row', axis=0, tiled=True)  66.2 us
    reduce_scatter x1, waiting for transfers between devices, shards(): lax.psum_scatter(expand_grad.astype(jnp.bfloat16), 'row', scatter_dimensi...  65.7 us
    reduce_scatter x1, waiting for transfers between devices, shards(): lax.psum_scatter(heads_grad.astype(jnp.bfloat16), 'row', scatter_dimensio...  63.2 us
    unnamed x167, local copies, waits for them, and re-layouts  23.8 us
    all_gather x4, waiting for transfers between devices, norm_split(): lax.all_gather(normed, 'col', axis=1, tiled=True)  22.7 us
  transfers between devices with their start and end apart: 25, of which 15 were waited for; matrix products, arithmetic and copies ran while one was open for 30% of the time, Pallas kernels for 0%

commit v1 on v0

--- a/solution.py
+++ b/solution.py
@@ -118,7 +118,9 @@
     heads_full, merge_full, expand_full, shrink_full = (
         lax.all_gather(heads_weight, "row", axis=0, tiled=True),
         lax.all_gather(merge_weight, "row", axis=1, tiled=True),
-        lax.all_gather(expand_weight, "row", axis=0, tiled=True),
+        jnp.concatenate(
+            lax.all_to_all(jnp.stack([expand_weight] * lax.axis_size("row")), "row", 0, 0), axis=0
+        ),
         lax.all_gather(shrink_weight, "row", axis=1, tiled=True),
     )
     member = (micro_batch[:, None] == jnp.arange(MICRO, dtype=jnp.int32)[None, :]).astype(jnp.int32)

time: 851 us -> 854 us (level)
  waiting for transfers between devices: 422 us -> 261 us
  blocking collectives: 107 us -> 258 us
    psum x1, blocking collectives: 14.7 us -> 165 us  [shards(): totals = lax.psum(jnp.sum(member, axis=0), ('dp', 'row'))]
    all_gather x1, waiting for transfers between devices: 75.9 us -> 0.01 us  [shards(): lax.all_gather(shrink_weight, 'row', axis=1, tiled=True)]
    all_gather x1 -> x0, waiting for transfers between devices: 74.1 us -> none  [shards(): lax.all_gather(expand_weight, 'row', axis=0, tiled=True)]
    all_gather x4, waiting for transfers between devices: 22.7 us -> 13.5 us  [norm_split(): lax.all_gather(normed, 'col', axis=1, tiled=True)]
    unnamed x167 -> x169, local copies, waits for them, and re-layouts: 23.8 us -> 24.4 us
  transfers between devices with their start and end apart: 25 -> 25, of which waited for: 15 -> 12; matrix products, arithmetic and copies ran while one was open for 30% -> 31% of each run, Pallas kernels for 0% -> 0%
where the time goes in v1:
time: 854 us; the launch traced here: 848 us
  waiting for transfers between devices  261 us (31%)
  blocking collectives  258 us (30%)
  matrix products  179 us (21%)
  local copies, waits for them, and re-layouts  63.3 us (7%)
  other arithmetic  63 us (7%)
  between operations  16.6 us (2%)
    psum x1, blocking collectives, shards(): totals = lax.psum(jnp.sum(member, axis=0), ('dp', 'row'))  165 us
    psum x1, blocking collectives, shards(): lax.psum((heads_bias_grad, merge_bias_grad, expand_bias_grad, shrink_bias...  78.2 us
    all_gather x1, waiting for transfers between devices, shards(): lax.all_gather(heads_weight, 'row', axis=0, tiled=True)  66.2 us
    reduce_scatter x1, waiting for transfers between devices, shards(): lax.psum_scatter(expand_grad.astype(jnp.bfloat16), 'row', scatter_dimensi...  65.7 us
    reduce_scatter x1, waiting for transfers between devices, shards(): lax.psum_scatter(heads_grad.astype(jnp.bfloat16), 'row', scatter_dimensio...  63.2 us
    unnamed x169, local copies, waits for them, and re-layouts  24.4 us
    reduce_scatter x4, waiting for transfers between devices, norm_back_split(): lax.psum_scatter(partial_rows.astype(jnp.bfloat16), 'col', scatter_dimens...  21.8 us
  transfers between devices with their start and end apart: 25, of which 12 were waited for; matrix products, arithmetic and copies ran while one was open for 31% of the time, Pallas kernels for 0%

profile of v1, /device:TPU:0, one launch (start us, length us, event | category | flops | bytes accessed | tf_op | source)
XLA Modules:
  0.0 847.7 jit_solution(6610414985704828692)
XLA Ops:
  26.4 9.3 %all-gather.32.cloned.1.call-done = bf16[577,1024]{1,0:T(8,128)(2,1)} async-done(((bf16[577,512]{1,0:T(8,128)(2,1)}), bf16[577,1024]{1,0:T(8,128)(2,1)}) %all-gather.32.cloned.1.call-update) | async-done | bytes 1181712 | tf_op jit(solution)/shard_map/all_gather | solution.py:36
  35.7 66.2 %all-gather.24.cloned.1.call-done = bf16[1024,3,512]{2,0,1:T(8,128)(2,1)} async-done(((bf16[256,3,512]{2,0,1:T(8,128)(2,1)}), bf16[1024,3,512]{2,0,1:T(8,128)(2,1)}) %all-gather.24.cloned.1.call-update) | async-done | bytes 3145744 | tf_op jit(solution)/shard_map/all_gather | solution.py:119
  122.0 6.5 fusion.145
  138.0 6.2 exponential_reduce_fusion
  194.2 165.4 %psum.133 = s32[2]{0:T(128)S(1)} all-reduce(s32[2]{0:T(128)S(1)} %fusion.120), channel_id=1, replica_groups=mesh['dp'=4,'row'=4,'col'=2] {'dp','row'}, use_global_device_ids=true, to_apply=%region_17.18 | all-reduce | flops 2 | bytes 16 | tf_op jit(solution)/shard_map/psum | solution.py:127
  368.9 7.5 fusion.147
  376.4 8.5 %convert_reduce_fusion = (f32[2048]{0:T(1024)}, bf16[577,2048]{1,0:T(8,128)(2,1)S(1)}) fusion(f32[577,2048]{1,0:T(8,128)} %fusion.147, f32[2048]{0:T(1024)S(1)} %convert_element_type.388, bf16[2048,1024]{1,0:T(8,128)(2,1)} %all-gather.30.cloned.1.call-done, bf16[1,577,1024]{2,1,0:T(8,128)(2,1)} %get-tuple-element.297), kind=kOutput, calls=%fused_computation.13 | convolution fusion | flops 2435473408 | bytes 12482560 | tf_op jit(solution)/shard_map/td,fd->tf/dot_general | solution.py:195
  386.4 6.0 convolution_convert_fusion
  404.0 6.0 convolution_convert_fusion.1
  410.1 7.7 convolution_convert_fusion.4
  417.9 7.3 convolution_convert_fusion.2
  442.8 8.8 %all-gather.36.cloned.1.call-done = bf16[577,1024]{1,0:T(8,128)(2,1)} async-done(((bf16[577,512]{1,0:T(8,128)(2,1)}), bf16[577,1024]{1,0:T(8,128)(2,1)}) %all-gather.36.cloned.1.call-update) | async-done | bytes 1181712 | tf_op jit(solution)/shard_map/all_gather | solution.py:54
  455.4 8.1 all-gather.38.cloned.1.call-done
  473.1 8.0 add_convert_fusion
  500.7 7.3 fusion.31
  509.1 7.3 fusion.37
  518.6 6.0 multiply_reduce_fusion
  524.7 6.1 multiply_convert_fusion
  547.4 6.1 multiply_convert_fusion.1
  587.5 65.7 %reduce-scatter.33.cloned.1.call-done = bf16[256,2048]{1,0:T(8,128)(2,1)} async-done(((bf16[1024,2048]{1,0:T(8,128)(2,1)}), bf16[256,2048]{1,0:T(8,128)(2,1)}) %reduce-scatter.33.cloned.1.call-update) | async-done | bytes 1048592 | tf_op jit(solution)/shard_map/reduce_scatter | solution.py:261
  653.2 63.2 %reduce-scatter.29.cloned.1.call-done = bf16[256,3,512]{2,0,1:T(8,128)(2,1)} async-done(((bf16[1024,3,512]{2,0,1:T(8,128)(2,1)}), bf16[256,3,512]{2,0,1:T(8,128)(2,1)}) %reduce-scatter.29.cloned.1.call-update) | async-done | bytes 786448 | tf_op jit(solution)/shard_map/reduce_scatter | solution.py:255
  719.0 9.0 %reduce-scatter.27.cloned.1.call-done = bf16[577,512]{1,0:T(8,128)(2,1)} async-done(((bf16[577,1024]{1,0:T(8,128)(2,1)}), bf16[577,512]{1,0:T(8,128)(2,1)}) %reduce-scatter.27.cloned.1.call-update) | async-done | bytes 590864 | tf_op jit(solution)/shard_map/reduce_scatter | solution.py:40
  728.0 12.7 %reduce-scatter.23.cloned.1.call-done = bf16[577,512]{1,0:T(8,128)(2,1)} async-done(((bf16[577,1024]{1,0:T(8,128)(2,1)}), bf16[577,512]{1,0:T(8,128)(2,1)}) %reduce-scatter.23.cloned.1.call-update) | async-done | bytes 590864 | tf_op jit(solution)/shard_map/reduce_scatter | solution.py:40
  752.7 78.2 %all-reduce.8 = (f32[2,512]{1,0:T(2,128)}, f32[512]{0:T(512)}, f32[2048]{0:T(1024)}, f32[512]{0:T(512)}, f32[2,512]{1,0:T(2,128)}, /*index=5*/f32[2,512]{1,0:T(2,128)}) all-reduce(f32[2,512]{1,0:T(2,128)S(1)} %maximum_add_fusion, f32[512]{0:T(512)S(1)} %add.530, ...), channel_id=1, replica_groups=mesh['dp'=4,'row'=4,'col'=2] {'dp','row'}, use_global_device_ids=true, to_apply=%region_47.48 | all-reduce | flops 6144 | bytes 49152 | tf_op jit(solution)/shard_map/psum | solution.py:274
  (361 shorter events, 247.6 us)
Async XLA Ops:
  7.2 28.5 %all-gather.32.cloned.1.call-start = ((), (), s32[]{:S(2)}) async-start(), calls=%async_computation.20 | async-start | bytes 1794048 | tf_op jit(solution)/shard_map/all_gather | solution.py:36
  23.9 78.1 %all-gather.24.cloned.1.call-start = ((), (), s32[]{:S(2)}) async-start(), calls=%async_computation.14 | async-start | bytes 3932160 | tf_op jit(solution)/shard_map/all_gather | solution.py:119
  24.6 87.4 %all-gather.22.cloned.1.call-start = ((), (), s32[]{:S(2)}) async-start(), calls=%async_computation.13 | async-start | bytes 1794048 | tf_op jit(solution)/shard_map/all_gather | solution.py:36
  25.3 124.7 %all-gather.26.cloned.1.call-start = ((), (), s32[]{:S(2)}) async-start(), calls=%async_computation.15 | async-start | bytes 1310720 | tf_op jit(solution)/shard_map/all_gather | solution.py:120
  25.9 146.4 %reduce-scatter.17.cloned.1.call-start = ((), (), s32[]{:S(2)}) async-start(), calls=%async_computation.21 | async-start | bytes 1794048 | tf_op jit(solution)/shard_map/reduce_scatter | solution.py:58
  153.4 23.1 %reduce-scatter.13.cloned.1.call-start = ((), (), s32[]{:S(2)}) async-start(), calls=%async_computation.16 | async-start | bytes 1794048 | tf_op jit(solution)/shard_map/reduce_scatter | solution.py:58
  166.5 193.9 %all-gather.40.cloned.1.call-start = ((), (), s32[]{:S(2)}) async-start(), calls=%async_computation.34 | async-start | bytes 1794048 | tf_op jit(solution)/shard_map/all_gather | solution.py:54
  171.2 193.3 %all-gather.42.cloned.1.call-start = ((), (), s32[]{:S(2)}) async-start(), calls=%async_computation.35 | async-start | bytes 1794048 | tf_op jit(solution)/shard_map/all_gather | solution.py:54
  172.3 196.6 %all-gather.34.cloned.1.call-start = ((), (), s32[]{:S(2)}) async-start(), calls=%async_computation.22 | async-start | bytes 1794048 | tf_op jit(solution)/shard_map/all_gather | solution.py:36
  185.2 191.2 %all-gather.30.cloned.1.call-start = ((), (), s32[]{:S(2)}) async-start(), calls=%async_computation.18 | async-start | bytes 5242880 | tf_op jit(solution)/shard_map/all_gather | solution.py:124
  189.0 179.8 %all-to-all-start = ((bf16[4,256,2048]{2,1,0:T(8,128)(2,1)}), bf16[4,256,2048]{2,1,0:T(8,128)(2,1)}, u32[]{:S(2)}, u32[]{:S(2)}) async-start(bf16[4,256,2048]{2,1,0:T(8,128)(2,1)} %stack.57), calls=%async_computation.1 | async-start | bytes 8388608 | tf_op jit(solution)/shard_map/all_to_all | solution.py:122
  194.1 198.6 %all-gather.28.cloned.1.call-start = ((), (), s32[]{:S(2)}) async-start(), calls=%async_computation.17 | async-start | bytes 1794048 | tf_op jit(solution)/shard_map/all_gather | solution.py:36
  368.8 56.6 %reduce-scatter.25.cloned.1.call-start = ((), (), s32[]{:S(2)}) async-start(), calls=%async_computation.27 | async-start | bytes 1794048 | tf_op jit(solution)/shard_map/reduce_scatter | solution.py:40
  392.4 32.9 %reduce-scatter.21.cloned.1.call-start = ((), (), s32[]{:S(2)}) async-start(), calls=%async_computation.24 | async-start | bytes 1794048 | tf_op jit(solution)/shard_map/reduce_scatter | solution.py:40
  410.0 22.0 %reduce-scatter.15.cloned.1.call-start = ((), (), s32[]{:S(2)}) async-start(), calls=%async_computation.19 | async-start | bytes 1794048 | tf_op jit(solution)/shard_map/reduce_scatter | solution.py:58
  425.3 26.4 %all-gather.36.cloned.1.call-start = ((), (), s32[]{:S(2)}) async-start(), calls=%async_computation.25 | async-start | bytes 1794048 | tf_op jit(solution)/shard_map/all_gather | solution.py:54
  435.9 27.6 %all-gather.38.cloned.1.call-start = ((), (), s32[]{:S(2)}) async-start(), calls=%async_computation.28 | async-start | bytes 1794048 | tf_op jit(solution)/shard_map/all_gather | solution.py:54
  442.7 144.7 %reduce-scatter.31.cloned.1.call-start = ((), (), s32[]{:S(2)}) async-start(), calls=%async_computation.31 | async-start | bytes 1310720 | tf_op jit(solution)/shard_map/reduce_scatter | solution.py:258
  467.4 120.0 %reduce-scatter.35.cloned.1.call-start = ((), (), s32[]{:S(2)}) async-start(), calls=%async_computation.33 | async-start | bytes 5242880 | tf_op jit(solution)/shard_map/reduce_scatter | solution.py:264
  481.2 172.0 %reduce-scatter.33.cloned.1.call-start = ((), (), s32[]{:S(2)}) async-start(), calls=%async_computation.32 | async-start | bytes 5242880 | tf_op jit(solution)/shard_map/reduce_scatter | solution.py:261
  492.4 223.9 %reduce-scatter.29.cloned.1.call-start = ((), (), s32[]{:S(2)}) async-start(), calls=%async_computation.30 | async-start | bytes 3932160 | tf_op jit(solution)/shard_map/reduce_scatter | solution.py:255
  571.4 156.7 %reduce-scatter.27.cloned.1.call-start = ((), (), s32[]{:S(2)}) async-start(), calls=%async_computation.29 | async-start | bytes 1794048 | tf_op jit(solution)/shard_map/reduce_scatter | solution.py:40
  576.8 164.0 %reduce-scatter.23.cloned.1.call-start = ((), (), s32[]{:S(2)}) async-start(), calls=%async_computation.26 | async-start | bytes 1794048 | tf_op jit(solution)/shard_map/reduce_scatter | solution.py:40
  582.2 251.9 %all-reduce.16.cloned.1.call-start = ((), (), s32[]{:S(2)}) async-start(), calls=%async_computation.36 | async-start | bytes 6291456 | tf_op jit(solution)/shard_map/psum | solution.py:269
  (77 other events, 944.7 us)
Sparse Core Ops, SparseCore 0:
  24.0 11.6 all-gather.31
  37.3 64.6 all-gather.23
  104.1 7.9 all-gather.21
  113.4 31.3 all-gather.25
  153.5 9.7 reduce-scatter.16
  166.7 9.7 reduce-scatter.12
  178.0 10.4 all-gather.39
  190.1 10.4 all-gather.41
  202.1 10.4 all-gather.33
  213.9 141.7 all-gather.29
  368.9 5.5 all-gather.27
  392.6 4.9 reduce-scatter.24
  410.1 4.8 reduce-scatter.20
  417.9 9.0 reduce-scatter.14
  429.2 9.8 reduce-scatter.18
  441.1 10.4 all-gather.35
  453.0 10.4 all-gather.37
  467.5 28.3 reduce-scatter.30
  498.3 75.4 reduce-scatter.34
  575.9 77.2 reduce-scatter.32
  655.6 60.7 reduce-scatter.28
  719.3 8.6 reduce-scatter.26
  730.9 9.8 reduce-scatter.22
  744.4 89.6 all-reduce.15
